TPU v7x, 32 devices: a whole 2x2x4 slice. The times are simulated.
32 devices in a mesh: dp: 8 (over z, y), tensor: 4 (over x, core).
Axes of the slice: x: 2, y: 2, z: 4, core: 2. Of those that a mesh axis runs over, the one named last changes fastest.
Arguments:
- tokens: bfloat16 [8192, 1024], P('dp', 'tensor'), may hold values from -6 to 6
- dealing: int32 [8192], P('dp'), may hold values from 0 to 8191, as said below
- seq_ids: int32 [8192], P('dp'), may hold values from 0 to 8191, as said below
- first_values: bfloat16 [8192, 1024], P('dp', 'tensor'), may hold values from -6 to 6
- out_grad: bfloat16 [8192, 1024], P('dp', 'tensor'), may hold values from -6 to 6
- norm1_gain: bfloat16 [1024], replicated, may hold values from 0.5 to 1.5
- norm2_gain: bfloat16 [1024], replicated, may hold values from 0.5 to 1.5
- w_query: bfloat16 [1024, 1024], P(None, 'tensor'), may hold values from -0.1875 to 0.1875
- w_key: bfloat16 [1024, 1024], P(None, 'tensor'), may hold values from -0.1875 to 0.1875
- w_value: bfloat16 [1024, 1024], P(None, 'tensor'), may hold values from -0.1875 to 0.1875
- w_out: bfloat16 [1024, 1024], P('tensor'), may hold values from -1 to 1
- w_gate: bfloat16 [1024, 2816], P(None, 'tensor'), may hold values from -0.1875 to 0.1875
- w_up: bfloat16 [1024, 2816], P(None, 'tensor'), may hold values from -0.1875 to 0.1875
- w_down: bfloat16 [2816, 1024], P('tensor'), may hold values from -0.109375 to 0.109375
Outputs:
- output: bfloat16 [8192, 1024], P('dp', 'tensor')
- input_grad: bfloat16 [8192, 1024], P('dp', 'tensor')
- first_values_grad: bfloat16 [8192, 1024], P('dp', 'tensor')
- norm1_gain_grad: float32 [4, 256], P('tensor', 'dp')
- norm2_gain_grad: float32 [4, 256], P('tensor', 'dp')
- w_query_grad: float32 [1024, 1024], P('dp', 'tensor')
- w_key_grad: float32 [1024, 1024], P('dp', 'tensor')
- w_value_grad: float32 [1024, 1024], P('dp', 'tensor')
- w_out_grad: float32 [1024, 1024], P('tensor', 'dp')
- w_gate_grad: float32 [1024, 2816], P('dp', 'tensor')
- w_up_grad: float32 [1024, 2816], P('dp', 'tensor')
- w_down_grad: float32 [2816, 1024], P('tensor', 'dp')
Inputs may be any that keep to these rules, and one draw needn't show every extreme that they name: `dealing`: a permutation; the tokens of each dp index go evenly, 1024 / 8 of them, to the rows of each dp index's block of 1024 dealt rows. `seq_ids`: never fall; no sequence crosses a multiple of 1024 rows; in every draw some block of 1024 rows is a single sequence; the rows of block b carry ids from b * 1024 to b * 1024 + 1023.
All inputs are finite; a program needn't handle non-finite values.
Results may differ from a plain program's by a relative error of at most 0.013.
Values may be sent and summed in bfloat16 or wider, within the bound.
No kernel may reach another device: no remote copies, remote signals or barrier semaphores. Data moves between devices by JAX's collectives and lax.ppermute only.
A program may use at most 128 MiB of HBM per device.

v0:
```python
import jax
import jax.numpy as jnp
from jax import lax
from jax.sharding import PartitionSpec as P

HEAD_DIM = 64
EPS = 1e-06
THETA = 10000.0
NEG = -1e30


def rope_tables(seq_row, head_dim):
    count = seq_row.shape[0]
    places = jnp.arange(count, dtype=jnp.int32)
    change = jnp.concatenate([jnp.ones((1,), bool), seq_row[1:] != seq_row[:-1]])
    starts = lax.cummax(jnp.where(change, places, jnp.zeros_like(places)), axis=0)
    offset = (places - starts).astype(jnp.float32)
    half = head_dim // 2
    freqs = THETA ** (-jnp.arange(half, dtype=jnp.float32) / half)
    angles = offset[:, None] * freqs[None, :]
    return (jnp.cos(angles), jnp.sin(angles))


def rotate(values, cos_rows, sin_rows):
    count = values.shape[0]
    half = cos_rows.shape[1]
    parts = values.reshape(count, -1, 2, half)
    first = parts[:, :, 0]
    second = parts[:, :, 1]
    cos_b = cos_rows[:, None, :]
    sin_b = sin_rows[:, None, :]
    return jnp.stack(
        [first * cos_b - second * sin_b, second * cos_b + first * sin_b], axis=2
    ).reshape(count, -1)


def rotate_back(grads, cos_rows, sin_rows):
    count = grads.shape[0]
    half = cos_rows.shape[1]
    parts = grads.reshape(count, -1, 2, half)
    first = parts[:, :, 0]
    second = parts[:, :, 1]
    cos_b = cos_rows[:, None, :]
    sin_b = sin_rows[:, None, :]
    return jnp.stack(
        [first * cos_b + second * sin_b, second * cos_b - first * sin_b], axis=2
    ).reshape(count, -1)


def row_total(values):
    return lax.psum(values, "tensor")


def gather_normed(normed):
    return lax.all_gather(normed, "tensor", axis=1, tiled=True)


def branch_sum(term):
    return lax.psum_scatter(term, "tensor", scatter_dimension=1, tiled=True)


def gather_grad(grads):
    return lax.all_gather(grads, "tensor", axis=1, tiled=True)


def input_sum(term):
    return lax.psum_scatter(term, "tensor", scatter_dimension=1, tiled=True)


def norm_forward(resid, gain):
    width = resid.shape[1] * lax.axis_size("tensor")
    total = row_total(jnp.sum(resid * resid, axis=1))
    scale = lax.rsqrt(total / width + EPS)[:, None]
    normed = (resid * scale * gain).astype(jnp.bfloat16)
    return (gather_normed(normed), scale)


def norm_backward(dnormed, resid, scale, gain):
    width = resid.shape[1] * lax.axis_size("tensor")
    weighted = dnormed * gain
    dot_row = row_total(jnp.sum(weighted * resid, axis=1))[:, None]
    dresid = scale * weighted - resid * (scale * scale * scale) * dot_row / width
    dgain = jnp.sum(dnormed * resid * scale, axis=0)
    return (dresid, dgain)


def block_mask(seq_block, seq_row, start):
    block = seq_block.shape[0]
    count = seq_row.shape[0]
    rows = start + jnp.arange(block, dtype=jnp.int32)
    cols = jnp.arange(count, dtype=jnp.int32)
    return (seq_block[:, None] == seq_row[None, :]) & (cols[None, :] <= rows[:, None])


def attend(queries, keys, values, seq_row, block):
    count, heads, depth = queries.shape
    blocks = count // block
    factor = depth ** (-0.5)
    query_blocks = queries.reshape(blocks, block, heads, depth)
    seq_blocks = seq_row.reshape(blocks, block)
    starts = jnp.arange(blocks, dtype=jnp.int32) * block

    def one_block(items):
        query_block, seq_block, start = items
        scores = (
            jnp.einsum("qhd,khd->hqk", query_block, keys, preferred_element_type=jnp.float32)
            * factor
        )
        mask = block_mask(seq_block, seq_row, start)
        scores = jnp.where(mask[None], scores, NEG)
        top = jnp.max(scores, axis=-1, keepdims=True)
        expo = jnp.exp(scores - top)
        total = jnp.sum(expo, axis=-1, keepdims=True)
        probs = expo / total
        result = jnp.einsum(
            "hqk,khd->qhd", probs.astype(jnp.bfloat16), values, preferred_element_type=jnp.float32
        )
        return (result.astype(jnp.bfloat16), (top + jnp.log(total))[:, :, 0])

    results, log_totals = lax.map(one_block, (query_blocks, seq_blocks, starts))
    return (results.reshape(count, heads * depth), log_totals)


def attend_back(queries, keys, values, seq_row, log_totals, dattn, block):
    count, heads, depth = queries.shape
    blocks = count // block
    factor = depth ** (-0.5)
    query_blocks = queries.reshape(blocks, block, heads, depth)
    seq_blocks = seq_row.reshape(blocks, block)
    grad_blocks = dattn.reshape(blocks, block, heads, depth)
    starts = jnp.arange(blocks, dtype=jnp.int32) * block

    def one_back(carry, items):
        dkey_acc, dval_acc = carry
        query_block, seq_block, start, log_block, grad_block = items
        scores = (
            jnp.einsum("qhd,khd->hqk", query_block, keys, preferred_element_type=jnp.float32)
            * factor
        )
        mask = block_mask(seq_block, seq_row, start)
        probs = jnp.where(mask[None], jnp.exp(scores - log_block[:, :, None]), 0.0)
        dval_acc = dval_acc + jnp.einsum(
            "hqk,qhd->khd",
            probs.astype(jnp.bfloat16),
            grad_block,
            preferred_element_type=jnp.float32,
        )
        dprob = jnp.einsum("qhd,khd->hqk", grad_block, values, preferred_element_type=jnp.float32)
        delta = jnp.sum(probs * dprob, axis=-1, keepdims=True)
        dscore = (probs * (dprob - delta)).astype(jnp.bfloat16)
        dquery = (
            jnp.einsum("hqk,khd->qhd", dscore, keys, preferred_element_type=jnp.float32) * factor
        )
        dkey_acc = (
            dkey_acc
            + jnp.einsum("hqk,qhd->khd", dscore, query_block, preferred_element_type=jnp.float32)
            * factor
        )
        return ((dkey_acc, dval_acc), dquery)

    zeros = jnp.zeros((count, heads, depth), jnp.float32)
    (dkeys, dvals), dqueries = lax.scan(
        one_back, (zeros, zeros), (query_blocks, seq_blocks, starts, log_totals, grad_blocks)
    )
    return (
        dqueries.reshape(count, heads * depth),
        dkeys.reshape(count, heads * depth),
        dvals.reshape(count, heads * depth),
    )


def per_device(
    tokens,
    dealing,
    seq_ids,
    first_values,
    out_grad,
    norm1_gain,
    norm2_gain,
    w_query,
    w_key,
    w_value,
    w_out,
    w_gate,
    w_up,
    w_down,
):
    order = jnp.argsort(dealing)
    arrived = (
        lax.all_to_all(tokens[order], "dp", split_axis=0, concat_axis=0, tiled=True),
        lax.all_to_all(first_values[order], "dp", split_axis=0, concat_axis=0, tiled=True),
        lax.all_to_all(out_grad[order], "dp", split_axis=0, concat_axis=0, tiled=True),
        lax.all_to_all(dealing[order], "dp", split_axis=0, concat_axis=0, tiled=True),
    )
    in_rows, in_first, in_grad, in_slots = arrived
    count = in_rows.shape[0]
    local_slot = in_slots % count
    arrange = jnp.argsort(local_slot)
    resid = in_rows[arrange].astype(jnp.float32)
    first_rows = in_first[arrange].astype(jnp.float32)
    grad_bf = in_grad[arrange]
    shard = resid.shape[1]
    rank = lax.axis_index("tensor")
    gain1 = lax.dynamic_slice_in_dim(norm1_gain, rank * shard, shard).astype(jnp.float32)
    gain2 = lax.dynamic_slice_in_dim(norm2_gain, rank * shard, shard).astype(jnp.float32)
    cos_rows, sin_rows = rope_tables(seq_ids, HEAD_DIM)
    heads = w_query.shape[1] // HEAD_DIM
    block = min(512, count)
    normed1, scale1 = norm_forward(resid, gain1)
    query_pre = jnp.dot(normed1, w_query, preferred_element_type=jnp.float32)
    key_pre = jnp.dot(normed1, w_key, preferred_element_type=jnp.float32)
    value_pre = jnp.dot(normed1, w_value, preferred_element_type=jnp.float32)
    queries = (
        rotate(query_pre, cos_rows, sin_rows).astype(jnp.bfloat16).reshape(count, heads, HEAD_DIM)
    )
    keys = rotate(key_pre, cos_rows, sin_rows).astype(jnp.bfloat16).reshape(count, heads, HEAD_DIM)
    values = (
        (0.5 * value_pre + 0.5 * first_rows).astype(jnp.bfloat16).reshape(count, heads, HEAD_DIM)
    )
    attended, log_totals = attend(queries, keys, values, seq_ids, block)
    middle = resid + branch_sum(jnp.dot(attended, w_out, preferred_element_type=jnp.float32))
    normed2, scale2 = norm_forward(middle, gain2)
    gate = jnp.dot(normed2, w_gate, preferred_element_type=jnp.float32)
    upval = jnp.dot(normed2, w_up, preferred_element_type=jnp.float32)
    sigmoid = jax.nn.sigmoid(gate)
    hidden = (gate * sigmoid * upval).astype(jnp.bfloat16)
    result = (
        middle + branch_sum(jnp.dot(hidden, w_down, preferred_element_type=jnp.float32))
    ).astype(jnp.bfloat16)
    full_grad = gather_grad(grad_bf)
    grad_down = jnp.einsum("tf,td->fd", hidden, full_grad, preferred_element_type=jnp.float32)
    grad_hidden = jnp.einsum("td,fd->tf", full_grad, w_down, preferred_element_type=jnp.float32)
    grad_up = (grad_hidden * gate * sigmoid).astype(jnp.bfloat16)
    grad_gate = (grad_hidden * upval * sigmoid * (1.0 + gate * (1.0 - sigmoid))).astype(
        jnp.bfloat16
    )
    grad_wgate = jnp.einsum("td,tf->df", normed2, grad_gate, preferred_element_type=jnp.float32)
    grad_wup = jnp.einsum("td,tf->df", normed2, grad_up, preferred_element_type=jnp.float32)
    dnormed2 = input_sum(
        jnp.einsum("tf,df->td", grad_gate, w_gate, preferred_element_type=jnp.float32)
        + jnp.einsum("tf,df->td", grad_up, w_up, preferred_element_type=jnp.float32)
    )
    dmiddle_norm, dgain2 = norm_backward(dnormed2, middle, scale2, gain2)
    dmiddle = grad_bf.astype(jnp.float32) + dmiddle_norm
    full_attn_grad = gather_grad(dmiddle.astype(jnp.bfloat16))
    grad_wout = jnp.einsum(
        "tc,td->cd", attended, full_attn_grad, preferred_element_type=jnp.float32
    )
    dattn = jnp.einsum(
        "td,cd->tc", full_attn_grad, w_out, preferred_element_type=jnp.float32
    ).astype(jnp.bfloat16)
    dqueries, dkeys, dvals = attend_back(queries, keys, values, seq_ids, log_totals, dattn, block)
    dquery_pre = rotate_back(dqueries, cos_rows, sin_rows).astype(jnp.bfloat16)
    dkey_pre = rotate_back(dkeys, cos_rows, sin_rows).astype(jnp.bfloat16)
    half_dval = (0.5 * dvals.astype(jnp.bfloat16).astype(jnp.float32)).astype(jnp.bfloat16)
    grad_wquery = jnp.einsum("td,tc->dc", normed1, dquery_pre, preferred_element_type=jnp.float32)
    grad_wkey = jnp.einsum("td,tc->dc", normed1, dkey_pre, preferred_element_type=jnp.float32)
    grad_wvalue = jnp.einsum("td,tc->dc", normed1, half_dval, preferred_element_type=jnp.float32)
    dnormed1 = input_sum(
        jnp.einsum("tc,dc->td", dquery_pre, w_query, preferred_element_type=jnp.float32)
        + jnp.einsum("tc,dc->td", dkey_pre, w_key, preferred_element_type=jnp.float32)
        + jnp.einsum("tc,dc->td", half_dval, w_value, preferred_element_type=jnp.float32)
    )
    dresid_norm, dgain1 = norm_backward(dnormed1, resid, scale1, gain1)
    dresid = (dmiddle + dresid_norm).astype(jnp.bfloat16)
    summed = (
        lax.psum_scatter(grad_wquery, "dp", scatter_dimension=0, tiled=True),
        lax.psum_scatter(grad_wkey, "dp", scatter_dimension=0, tiled=True),
        lax.psum_scatter(grad_wvalue, "dp", scatter_dimension=0, tiled=True),
        lax.psum_scatter(grad_wout, "dp", scatter_dimension=1, tiled=True),
        lax.psum_scatter(grad_wgate, "dp", scatter_dimension=0, tiled=True),
        lax.psum_scatter(grad_wup, "dp", scatter_dimension=0, tiled=True),
        lax.psum_scatter(grad_down, "dp", scatter_dimension=1, tiled=True),
        lax.psum_scatter(dgain1[None, :], "dp", scatter_dimension=1, tiled=True),
        lax.psum_scatter(dgain2[None, :], "dp", scatter_dimension=1, tiled=True),
    )
    returned = (
        lax.all_to_all(result[local_slot], "dp", split_axis=0, concat_axis=0, tiled=True),
        lax.all_to_all(dresid[local_slot], "dp", split_axis=0, concat_axis=0, tiled=True),
        lax.all_to_all(half_dval[local_slot], "dp", split_axis=0, concat_axis=0, tiled=True),
    )
    restore = jnp.argsort(order)
    output = returned[0][restore]
    input_grad = returned[1][restore]
    first_grad = returned[2][restore]
    return (
        output,
        input_grad,
        first_grad,
        summed[7],
        summed[8],
        summed[0],
        summed[1],
        summed[2],
        summed[3],
        summed[4],
        summed[5],
        summed[6],
    )


def solution(mesh):
    in_specs = (
        P("dp", "tensor"),
        P("dp"),
        P("dp"),
        P("dp", "tensor"),
        P("dp", "tensor"),
        P(),
        P(),
        P(None, "tensor"),
        P(None, "tensor"),
        P(None, "tensor"),
        P("tensor", None),
        P(None, "tensor"),
        P(None, "tensor"),
        P("tensor", None),
    )
    out_specs = (
        P("dp", "tensor"),
        P("dp", "tensor"),
        P("dp", "tensor"),
        P("tensor", "dp"),
        P("tensor", "dp"),
        P("dp", "tensor"),
        P("dp", "tensor"),
        P("dp", "tensor"),
        P("tensor", "dp"),
        P("dp", "tensor"),
        P("dp", "tensor"),
        P("tensor", "dp"),
    )
    return jax.shard_map(
        per_device, mesh=mesh, in_specs=in_specs, out_specs=out_specs, check_vma=False
    )
```

profile of v0, /device:TPU:0, one launch (start us, length us, event | category | flops | bytes accessed | tf_op | source)
XLA Modules:
  0.0 1110.9 jit_solution(10349196735572572018)
XLA Ops:
  12.4 8.8 gather_fusion.1
  21.3 7.3 all-to-all-start.1
  44.8 8.8 all-to-all-done
  77.3 10.9 all-to-all-done.2
  100.1 20.7 %while.27 = (s32[]{:T(128)}, bf16[2,512,4,64]{1,3,2,0:T(8,128)(2,1)}, f32[2,4,512]{2,1,0:T(4,128)}, s32[2,512]{1,0:T(2,128)S(1)}, s32[1024]{0:T(1024)S(1)}, /*in...) while((s32[]{:T(128)}, ...), condition=%wide.region_9.10_spmd, body=%wide.region_6.9_spmd.sunk | while | flops 563739136 | bytes 33241340 | solution.py:120
  128.7 42.2 %reduce-scatter.18.cloned.1.call-done = f32[1024,256]{1,0:T(8,128)} async-done(((f32[1024,1024]{1,0:T(8,128)}), f32[1024,256]{1,0:T(8,128)}) %reduce-scatter.18.cloned.1.call-update) | async-done | bytes 1048592 | tf_op jit(solution)/shard_map/reduce_scatter | solution.py:59
  186.9 20.0 %all_to_all.87 = bf16[8,128,256]{2,1,0:T(8,128)(2,1)S(1)} all-to-all(bf16[8,128,256]{2,1,0:T(8,128)(2,1)} %bitcast.210), channel_id=1, replica_groups=mesh['dp'=8,'tensor'=4] {'dp'}, dimensions={0} | all-to-all | bytes 1048576 | tf_op jit(solution)/shard_map/all_to_all | solution.py:192
  221.1 12.1 %all-gather.12.cloned.1.call-done = bf16[1024,1024]{1,0:T(8,128)(2,1)} async-done(((bf16[1024,256]{1,0:T(8,128)(2,1)}), bf16[1024,1024]{1,0:T(8,128)(2,1)}) %all-gather.12.cloned.1.call-update) | async-done | bytes 2097168 | tf_op jit(solution)/shard_map/all_gather | solution.py:63
  233.2 6.3 multiply_convert_fusion.1
  251.3 39.3 %reduce-scatter.22.cloned.1.call-done = f32[1024,256]{1,0:T(8,128)} async-done(((f32[1024,1024]{1,0:T(8,128)}), f32[1024,256]{1,0:T(8,128)}) %reduce-scatter.22.cloned.1.call-update) | async-done | bytes 1048592 | tf_op jit(solution)/shard_map/reduce_scatter | solution.py:67
  298.0 39.5 %reduce-scatter.20.cloned.1.call-done = f32[1024,256]{1,0:T(8,128)} async-done(((f32[1024,1024]{1,0:T(8,128)}), f32[1024,256]{1,0:T(8,128)}) %reduce-scatter.20.cloned.1.call-update) | async-done | bytes 1048592 | tf_op jit(solution)/shard_map/reduce_scatter | solution.py:59
  341.2 22.7 %all-gather.10.cloned.1.call-done = bf16[1024,1024]{1,0:T(8,128)(2,1)} async-done(((bf16[1024,256]{1,0:T(8,128)(2,1)}), bf16[1024,1024]{1,0:T(8,128)(2,1)}) %all-gather.10.cloned.1.call-update) | async-done | bytes 2097168 | tf_op jit(solution)/shard_map/all_gather | solution.py:63
  372.2 55.5 %while.28 = (s32[]{:T(128)}, f32[1024,4,64]{0,2,1:T(8,128)S(1)}, f32[1024,4,64]{0,2,1:T(8,128)}, f32[2,512,4,64]{1,0,3,2:T(2,128)}, bf16[2,512,4,64]{1,3,2,0:T(8...) while((s32[]{:T(128)}, f32[1024,4,64]{0,2,1:T(8,128)S(1)}, ...), condition=%wide.region_20.21_spmd.clone, body=%wide.region_18.20_spmd.clone.sunk | while | flops 1376647680 | bytes 74520776 | solution.py:162
  389.1 10.4 dynamic_update_slice.20
  416.9 10.4 dynamic_update_slice.20
  437.5 43.8 %reduce-scatter.24.cloned.1.call-done = f32[1024,256]{1,0:T(8,128)} async-done(((f32[1024,1024]{1,0:T(8,128)}), f32[1024,256]{1,0:T(8,128)}) %reduce-scatter.24.cloned.1.call-update) | async-done | bytes 1048592 | tf_op jit(solution)/shard_map/reduce_scatter | solution.py:67
  571.7 39.8 %reduce-scatter.40.cloned.1.call-done = f32[32,1]{1,0:T(8,128)} async-done(((f32[256,1]{1,0:T(8,128)}), f32[32,1]{1,0:T(8,128)}) %reduce-scatter.40.cloned.1.call-update) | async-done | bytes 144
  617.8 69.2 %reduce-scatter.38.cloned.1.call-done = f32[704,128]{1,0:T(8,128)} async-done(((f32[704,1024]{1,0:T(8,128)}), f32[704,128]{1,0:T(8,128)}) %reduce-scatter.38.cloned.1.call-update) | async-done | bytes 360464 | tf_op jit(solution)/shard_map/reduce_scatter | solution.py:273
  686.9 75.3 %reduce-scatter.36.cloned.1.call-done = f32[128,704]{0,1:T(8,128)} async-done(((f32[1024,704]{0,1:T(8,128)}), f32[128,704]{0,1:T(8,128)}) %reduce-scatter.36.cloned.1.call-update) | async-done | bytes 360464 | tf_op jit(solution)/shard_map/reduce_scatter | solution.py:272
  762.3 75.5 %reduce-scatter.34.cloned.1.call-done = f32[128,704]{0,1:T(8,128)} async-done(((f32[1024,704]{0,1:T(8,128)}), f32[128,704]{0,1:T(8,128)}) %reduce-scatter.34.cloned.1.call-update) | async-done | bytes 360464 | tf_op jit(solution)/shard_map/reduce_scatter | solution.py:271
  837.7 66.9 %reduce-scatter.32.cloned.1.call-done = f32[256,128]{1,0:T(8,128)} async-done(((f32[256,1024]{1,0:T(8,128)}), f32[256,128]{1,0:T(8,128)}) %reduce-scatter.32.cloned.1.call-update) | async-done | bytes 131088 | tf_op jit(solution)/shard_map/reduce_scatter | solution.py:270
  904.6 66.6 %reduce-scatter.30.cloned.1.call-done = f32[128,256]{1,0:T(8,128)} async-done(((f32[1024,256]{1,0:T(8,128)}), f32[128,256]{1,0:T(8,128)}) %reduce-scatter.30.cloned.1.call-update) | async-done | bytes 131088 | tf_op jit(solution)/shard_map/reduce_scatter | solution.py:269
  971.2 66.3 %reduce-scatter.28.cloned.1.call-done = f32[128,256]{1,0:T(8,128)} async-done(((f32[1024,256]{1,0:T(8,128)}), f32[128,256]{1,0:T(8,128)}) %reduce-scatter.28.cloned.1.call-update) | async-done | bytes 131088 | tf_op jit(solution)/shard_map/reduce_scatter | solution.py:268
  1037.5 66.7 %reduce-scatter.26.cloned.1.call-done = f32[128,256]{1,0:T(8,128)} async-done(((f32[1024,256]{1,0:T(8,128)}), f32[128,256]{1,0:T(8,128)}) %reduce-scatter.26.cloned.1.call-update) | async-done | bytes 131088 | tf_op jit(solution)/shard_map/reduce_scatter | solution.py:267
  (311 shorter events, 286.5 us)
Async XLA Ops:
  21.3 13.7 %all-to-all-start.1 = ((s32[8,128,1]{1,2,0:T(1,128)}), s32[8,128,1]{1,2,0:T(1,128)S(1)}, u32[]{:S(2)}, u32[]{:S(2)}) async-start(s32[8,128,1]{1,2,0:T(1,128)} %bitcast.9), calls=%async_computation.1 | async-start | bytes 8192 | tf_op jit(solution)/shard_map/all_to_all | solution.py:193
  34.9 18.6 %all-to-all-start = ((bf16[8,128,256]{2,1,0:T(8,128)(2,1)}), bf16[8,128,256]{2,1,0:T(8,128)(2,1)S(1)}, u32[]{:S(2)}, u32[]{:S(2)}) async-start(bf16[8,128,256]{2,1,0:T(8,128)(2,1)} %bitcast.6), calls=%async_computation | async-start | bytes 1048576 | tf_op jit(solution)/shard_map/all_to_all | solution.py:190
  39.5 53.7 %all-gather.6.cloned.1.call-start = ((), (), s32[]{:S(2)}) async-start(), calls=%async_computation.20 | async-start | bytes 2621440 | tf_op jit(solution)/shard_map/all_gather | solution.py:55
  70.0 18.3 %all-to-all-start.2 = ((bf16[8,128,256]{2,1,0:T(8,128)(2,1)}), bf16[8,128,256]{2,1,0:T(8,128)(2,1)S(1)}, u32[]{:S(2)}, u32[]{:S(2)}) async-start(bf16[8,128,256]{2,1,0:T(8,128)(2,1)} %bitcast.16), calls=%async_computation.2 | async-start | bytes 1048576 | tf_op jit(solution)/shard_map/all_to_all | solution.py:191
  74.3 96.6 %reduce-scatter.18.cloned.1.call-start = ((), (), s32[]{:S(2)}) async-start(), calls=%async_computation.21 | async-start | bytes 5242880 | tf_op jit(solution)/shard_map/reduce_scatter | solution.py:59
  127.3 85.1 %all-gather.8.cloned.1.call-start = ((), (), s32[]{:S(2)}) async-start(), calls=%async_computation.22 | async-start | bytes 2621440 | tf_op jit(solution)/shard_map/all_gather | solution.py:55
  181.8 51.4 %all-gather.12.cloned.1.call-start = ((), (), s32[]{:S(2)}) async-start(), calls=%async_computation.34 | async-start | bytes 2621440 | tf_op jit(solution)/shard_map/all_gather | solution.py:63
  212.1 78.5 %reduce-scatter.22.cloned.1.call-start = ((), (), s32[]{:S(2)}) async-start(), calls=%async_computation.24 | async-start | bytes 5242880 | tf_op jit(solution)/shard_map/reduce_scatter | solution.py:67
  245.9 91.6 %reduce-scatter.20.cloned.1.call-start = ((), (), s32[]{:S(2)}) async-start(), calls=%async_computation.23 | async-start | bytes 5242880 | tf_op jit(solution)/shard_map/reduce_scatter | solution.py:59
  251.2 112.7 %all-gather.10.cloned.1.call-start = ((), (), s32[]{:S(2)}) async-start(), calls=%async_computation.25 | async-start | bytes 2621440 | tf_op jit(solution)/shard_map/all_gather | solution.py:63
  340.9 140.3 %reduce-scatter.24.cloned.1.call-start = ((), (), s32[]{:S(2)}) async-start(), calls=%async_computation.26 | async-start | bytes 5242880 | tf_op jit(solution)/shard_map/reduce_scatter | solution.py:67
  436.6 123.8 %reduce-scatter.42.cloned.1.call-start = ((), (), s32[]{:S(2)}) async-start(), calls=%async_computation.36 | async-start | bytes 147456
  437.5 174.0 %reduce-scatter.40.cloned.1.call-start = ((), (), s32[]{:S(2)}) async-start(), calls=%async_computation.35 | async-start | bytes 147456
  483.9 203.1 %reduce-scatter.38.cloned.1.call-start = ((), (), s32[]{:S(2)}) async-start(), calls=%async_computation.33 | async-start | bytes 3244032 | tf_op jit(solution)/shard_map/reduce_scatter | solution.py:273
  488.5 273.7 %reduce-scatter.36.cloned.1.call-start = ((), (), s32[]{:S(2)}) async-start(), calls=%async_computation.32 | async-start | bytes 3244032 | tf_op jit(solution)/shard_map/reduce_scatter | solution.py:272
  494.8 342.9 %reduce-scatter.34.cloned.1.call-start = ((), (), s32[]{:S(2)}) async-start(), calls=%async_computation.31 | async-start | bytes 3244032 | tf_op jit(solution)/shard_map/reduce_scatter | solution.py:271
  499.5 405.1 %reduce-scatter.32.cloned.1.call-start = ((), (), s32[]{:S(2)}) async-start(), calls=%async_computation.30 | async-start | bytes 1179648 | tf_op jit(solution)/shard_map/reduce_scatter | solution.py:270
  503.8 467.4 %reduce-scatter.30.cloned.1.call-start = ((), (), s32[]{:S(2)}) async-start(), calls=%async_computation.29 | async-start | bytes 1179648 | tf_op jit(solution)/shard_map/reduce_scatter | solution.py:269
  505.7 531.8 %reduce-scatter.28.cloned.1.call-start = ((), (), s32[]{:S(2)}) async-start(), calls=%async_computation.28 | async-start | bytes 1179648 | tf_op jit(solution)/shard_map/reduce_scatter | solution.py:268
  513.7 20.0 %all-to-all-start.3 = ((bf16[8,128,256]{2,1,0:T(8,128)(2,1)}), bf16[8,128,256]{2,1,0:T(8,128)(2,1)S(1)}, u32[]{:S(2)}, u32[]{:S(2)}) async-start(bf16[8,128,256]{2,1,0:T(8,128)(2,1)} %bitcast.209), calls=%async_computation.5 | async-start | bytes 1048576 | tf_op jit(solution)/shard_map/all_to_all | solution.py:278
  519.2 584.9 %reduce-scatter.26.cloned.1.call-start = ((), (), s32[]{:S(2)}) async-start(), calls=%async_computation.27 | async-start | bytes 1179648 | tf_op jit(solution)/shard_map/reduce_scatter | solution.py:267
  533.7 18.6 %all-to-all-start.6 = ((bf16[8,128,256]{2,1,0:T(8,128)(2,1)}), bf16[8,128,256]{2,1,0:T(8,128)(2,1)S(1)}, u32[]{:S(2)}, u32[]{:S(2)}) async-start(bf16[8,128,256]{2,1,0:T(8,128)(2,1)} %bitcast.31), calls=%async_computation.10 | async-start | bytes 1048576 | tf_op jit(solution)/shard_map/all_to_all | solution.py:280
  552.3 60.5 %all-to-all-start.5 = ((bf16[8,128,256]{2,1,0:T(8,128)(2,1)}), bf16[8,128,256]{2,1,0:T(8,128)(2,1)S(1)}, u32[]{:S(2)}, u32[]{:S(2)}) async-start(bf16[8,128,256]{2,1,0:T(8,128)(2,1)} %bitcast.29), calls=%async_computation.9 | async-start | bytes 1048576 | tf_op jit(solution)/shard_map/all_to_all | solution.py:279
  566.7 537.5 %copy-start.1 = (bf16[704,1024]{1,0:T(8,128)(2,1)S(1)}, bf16[704,1024]{1,0:T(8,128)(2,1)}, u32[]{:S(2)}) copy-start(bf16[704,1024]{1,0:T(8,128)(2,1)} %param.31) | copy-start | bytes 4325380
  (64 other events, 1202.8 us)
Sparse Core Ops, SparseCore 0:
  65.1 22.1 all-gather.5
  127.4 43.4 reduce-scatter.17
  181.9 23.9 all-gather.7
  212.2 20.9 all-gather.11
  246.0 44.5 reduce-scatter.21
  293.0 44.4 reduce-scatter.19
  341.1 22.8 all-gather.9
  436.7 44.5 reduce-scatter.23
  484.6 62.1 reduce-scatter.41
  549.9 61.5 reduce-scatter.39
  615.6 71.2 reduce-scatter.37
  690.9 71.3 reduce-scatter.35
  766.4 71.2 reduce-scatter.33
  841.5 62.9 reduce-scatter.31
  908.8 62.3 reduce-scatter.29
  975.1 62.3 reduce-scatter.27
  1041.7 62.4 reduce-scatter.25
where the time goes:
time: 1120 us; the launch traced here: 1110 us
  waiting for transfers between devices  756 us (68%)
  local copies, waits for them, and re-layouts  114 us (10%)
  matrix products  102 us (9%)
  other arithmetic  50.5 us (5%)
  blocking collectives  43.2 us (4%)
  starting transfers between devices  30.6 us (3%)
  between operations  14.9 us (1%)
    reduce_scatter x2, waiting for transfers between devices, input_sum(): return lax.psum_scatter(term, 'tensor', scatter_dimension=1, tiled=True)  83.1 us
    reduce_scatter x2, waiting for transfers between devices, branch_sum(): return lax.psum_scatter(term, 'tensor', scatter_dimension=1, tiled=True)  81.7 us
    reduce_scatter x1, waiting for transfers between devices, per_device(): lax.psum_scatter(grad_wgate, 'dp', scatter_dimension=0, tiled=True)  75.5 us
    reduce_scatter x1, waiting for transfers between devices, per_device(): lax.psum_scatter(grad_wup, 'dp', scatter_dimension=0, tiled=True)  75.3 us
    reduce_scatter x1, waiting for transfers between devices, per_device(): lax.psum_scatter(grad_down, 'dp', scatter_dimension=1, tiled=True)  69.2 us
    reduce_scatter x1, waiting for transfers between devices, per_device(): lax.psum_scatter(grad_wout, 'dp', scatter_dimension=1, tiled=True)  66.9 us
    reduce_scatter x1, waiting for transfers between devices, per_device(): lax.psum_scatter(grad_wquery, 'dp', scatter_dimension=0, tiled=True)  66.7 us
    reduce_scatter x1, waiting for transfers between devices, per_device(): lax.psum_scatter(grad_wvalue, 'dp', scatter_dimension=0, tiled=True)  66.6 us
  transfers between devices with their start and end apart: 23, of which 19 were waited for; matrix products, arithmetic and copies ran while one was open for 11% of the time, Pallas kernels for 0%

commit v1 on v0

--- a/solution.py
+++ b/solution.py
@@ -7,6 +7,19 @@
 EPS = 1e-06
 THETA = 10000.0
 NEG = -1e30
+
+
+def gather_around(x, axis, dim):
+    ways = lax.axis_size(axis)
+    up = [(d, (d + 1) % ways) for d in range(ways)]
+    down = [(d, (d - 1) % ways) for d in range(ways)]
+    earlier, later = ([x], [x])
+    for _ in range(ways // 2):
+        earlier.append(lax.ppermute(earlier[-1], axis, up))
+    for _ in range((ways - 1) // 2):
+        later.append(lax.ppermute(later[-1], axis, down))
+    line = jnp.concatenate([*earlier[::-1], *later[1:]], axis=dim)
+    return jnp.roll(line, (lax.axis_index(axis) - ways // 2) * x.shape[dim], axis=dim)
 
 
 def rope_tables(seq_row, head_dim):
@@ -60,7 +73,7 @@
 
 
 def gather_grad(grads):
-    return lax.all_gather(grads, "tensor", axis=1, tiled=True)
+    return gather_around(grads, "tensor", 1)
 
 
 def input_sum(term):

time: 1120 us -> 1130 us (level)
    ppermute x0 -> x6, waiting for transfers between devices: none -> 41.2 us  [the longest x4 41.2 us: gather_around(): earlier.append(lax.ppermute(earlier[-1], axis, up))]
    all_gather x2 -> x0, waiting for transfers between devices: 34.8 us -> none  [gather_grad(): return lax.all_gather(grads, 'tensor', axis=1, tiled=True)]
    unnamed x19 -> x17, waiting for transfers between devices: 40.1 us -> 40.1 us
  transfers between devices with their start and end apart: 23 -> 27, of which waited for: 19 -> 21; matrix products, arithmetic and copies ran while one was open for 11% -> 10% of each run, Pallas kernels for 0% -> 0%
where the time goes in v1:
time: 1130 us; the launch traced here: 1120 us
  waiting for transfers between devices  760 us (67%)
  local copies, waits for them, and re-layouts  114 us (10%)
  matrix products  94.4 us (8%)
  other arithmetic  58.7 us (5%)
  blocking collectives  43.2 us (4%)
  starting transfers between devices  34 us (3%)
  between operations  15 us (1%)
    reduce_scatter x2, waiting for transfers between devices, branch_sum(): return lax.psum_scatter(term, 'tensor', scatter_dimension=1, tiled=True)  81.7 us
    reduce_scatter x2, waiting for transfers between devices, input_sum(): return lax.psum_scatter(term, 'tensor', scatter_dimension=1, tiled=True)  80.9 us
    reduce_scatter x1, waiting for transfers between devices, per_device(): lax.psum_scatter(grad_wgate, 'dp', scatter_dimension=0, tiled=True)  75.5 us
    reduce_scatter x1, waiting for transfers between devices, per_device(): lax.psum_scatter(grad_wup, 'dp', scatter_dimension=0, tiled=True)  75.3 us
    reduce_scatter x1, waiting for transfers between devices, per_device(): lax.psum_scatter(grad_down, 'dp', scatter_dimension=1, tiled=True)  69.2 us
    reduce_scatter x1, waiting for transfers between devices, per_device(): lax.psum_scatter(grad_wout, 'dp', scatter_dimension=1, tiled=True)  66.9 us
    reduce_scatter x1, waiting for transfers between devices, per_device(): lax.psum_scatter(grad_wvalue, 'dp', scatter_dimension=0, tiled=True)  66.9 us
    reduce_scatter x1, waiting for transfers between devices, per_device(): lax.psum_scatter(grad_wquery, 'dp', scatter_dimension=0, tiled=True)  66.7 us
  transfers between devices with their start and end apart: 27, of which 21 were waited for; matrix products, arithmetic and copies ran while one was open for 10% of the time, Pallas kernels for 0%

profile of v1, /device:TPU:0, one launch (start us, length us, event | category | flops | bytes accessed | tf_op | source)
XLA Modules:
  0.0 1120.3 jit_solution(9860333530502155369)
XLA Ops:
  12.4 8.8 gather_fusion.1
  44.8 8.8 all-to-all-done
  77.0 11.3 %all-to-all-done.2 = bf16[8,128,256]{2,1,0:T(8,128)(2,1)S(1)} async-done(((bf16[8,128,256]{2,1,0:T(8,128)(2,1)}), bf16[8,128,256]{2,1,0:T(8,128)(2,1)S(1)}, u32[]{:S(2)}, u32[]{:S(2)}) %all-to-all-start.2) | async-done | bytes 524320 | tf_op jit(solution)/shard_map/all_to_all | solution.py:204
  100.1 20.7 %while.27 = (s32[]{:T(128)}, bf16[2,512,4,64]{1,3,2,0:T(8,128)(2,1)}, f32[2,4,512]{2,1,0:T(4,128)}, s32[2,512]{1,0:T(2,128)S(1)}, s32[1024]{0:T(1024)S(1)}, /*in...) while((s32[]{:T(128)}, ...), condition=%wide.region_9.10_spmd, body=%wide.region_6.9_spmd.sunk | while | flops 563739136 | bytes 33241340 | solution.py:133
  128.6 42.2 %reduce-scatter.18.cloned.1.call-done = f32[1024,256]{1,0:T(8,128)} async-done(((f32[1024,1024]{1,0:T(8,128)}), f32[1024,256]{1,0:T(8,128)}) %reduce-scatter.18.cloned.1.call-update) | async-done | bytes 1048592 | tf_op jit(solution)/shard_map/reduce_scatter | solution.py:72
  186.9 19.9 %all_to_all.87 = bf16[8,128,256]{2,1,0:T(8,128)(2,1)S(1)} all-to-all(bf16[8,128,256]{2,1,0:T(8,128)(2,1)} %bitcast.210), channel_id=1, replica_groups=mesh['dp'=8,'tensor'=4] {'dp'}, dimensions={0} | all-to-all | bytes 1048576 | tf_op jit(solution)/shard_map/all_to_all | solution.py:205
  213.0 11.6 %collective-permute-done = bf16[1024,256]{1,0:T(8,128)(2,1)S(1)} collective-permute-done((bf16[1024,256]{1,0:T(8,128)(2,1)S(1)}, bf16[1024,256]{1,0:T(8,128)(2,1)S(1)}, u32[]{:S(2)}, u32[]{:S(2)}) %collective-permute-start) | collective-permute-done | bytes 524320 | tf_op jit(solution)/shard_map/ppermute | solution.py:18
  224.9 8.7 collective-permute-done.1
  259.4 37.4 %reduce-scatter.22.cloned.1.call-done = f32[1024,256]{1,0:T(8,128)} async-done(((f32[1024,1024]{1,0:T(8,128)}), f32[1024,256]{1,0:T(8,128)}) %reduce-scatter.22.cloned.1.call-update) | async-done | bytes 1048592 | tf_op jit(solution)/shard_map/reduce_scatter | solution.py:80
  304.2 39.5 %reduce-scatter.20.cloned.1.call-done = f32[1024,256]{1,0:T(8,128)} async-done(((f32[1024,1024]{1,0:T(8,128)}), f32[1024,256]{1,0:T(8,128)}) %reduce-scatter.20.cloned.1.call-update) | async-done | bytes 1048592 | tf_op jit(solution)/shard_map/reduce_scatter | solution.py:72
  348.6 12.0 %collective-permute-done.3 = bf16[1024,256]{1,0:T(8,128)(2,1)} collective-permute-done((bf16[1024,256]{1,0:T(8,128)(2,1)S(1)}, bf16[1024,256]{1,0:T(8,128)(2,1)}, u32[]{:S(2)}, u32[]{:S(2)}) %collective-permute-start.3) | collective-permute-done | bytes 524320 | tf_op jit(solution)/shard_map/ppermute | solution.py:18
  361.1 8.9 collective-permute-done.4
  381.7 55.2 %while.28 = (s32[]{:T(128)}, f32[1024,4,64]{0,2,1:T(8,128)S(1)}, f32[1024,4,64]{0,2,1:T(8,128)}, f32[2,512,4,64]{1,0,3,2:T(2,128)}, bf16[2,512,4,64]{1,3,2,0:T(8...) while((s32[]{:T(128)}, f32[1024,4,64]{0,2,1:T(8,128)S(1)}, ...), condition=%wide.region_20.22_spmd.clone, body=%wide.region_18.21_spmd.clone.sunk | while | flops 1376647680 | bytes 74520776 | solution.py:175
  398.7 10.4 dynamic_update_slice.20
  426.4 10.4 dynamic_update_slice.20
  446.8 43.5 %reduce-scatter.24.cloned.1.call-done = f32[1024,256]{1,0:T(8,128)} async-done(((f32[1024,1024]{1,0:T(8,128)}), f32[1024,256]{1,0:T(8,128)}) %reduce-scatter.24.cloned.1.call-update) | async-done | bytes 1048592 | tf_op jit(solution)/shard_map/reduce_scatter | solution.py:80
  580.6 39.9 %reduce-scatter.40.cloned.1.call-done = f32[32,1]{1,0:T(8,128)} async-done(((f32[256,1]{1,0:T(8,128)}), f32[32,1]{1,0:T(8,128)}) %reduce-scatter.40.cloned.1.call-update) | async-done | bytes 144
  626.8 69.2 %reduce-scatter.38.cloned.1.call-done = f32[704,128]{1,0:T(8,128)} async-done(((f32[704,1024]{1,0:T(8,128)}), f32[704,128]{1,0:T(8,128)}) %reduce-scatter.38.cloned.1.call-update) | async-done | bytes 360464 | tf_op jit(solution)/shard_map/reduce_scatter | solution.py:286
  696.0 75.3 %reduce-scatter.36.cloned.1.call-done = f32[128,704]{0,1:T(8,128)} async-done(((f32[1024,704]{0,1:T(8,128)}), f32[128,704]{0,1:T(8,128)}) %reduce-scatter.36.cloned.1.call-update) | async-done | bytes 360464 | tf_op jit(solution)/shard_map/reduce_scatter | solution.py:285
  771.3 75.5 %reduce-scatter.34.cloned.1.call-done = f32[128,704]{0,1:T(8,128)} async-done(((f32[1024,704]{0,1:T(8,128)}), f32[128,704]{0,1:T(8,128)}) %reduce-scatter.34.cloned.1.call-update) | async-done | bytes 360464 | tf_op jit(solution)/shard_map/reduce_scatter | solution.py:284
  846.8 66.9 %reduce-scatter.32.cloned.1.call-done = f32[256,128]{1,0:T(8,128)} async-done(((f32[256,1024]{1,0:T(8,128)}), f32[256,128]{1,0:T(8,128)}) %reduce-scatter.32.cloned.1.call-update) | async-done | bytes 131088 | tf_op jit(solution)/shard_map/reduce_scatter | solution.py:283
  913.7 66.9 %reduce-scatter.30.cloned.1.call-done = f32[128,256]{1,0:T(8,128)} async-done(((f32[1024,256]{1,0:T(8,128)}), f32[128,256]{1,0:T(8,128)}) %reduce-scatter.30.cloned.1.call-update) | async-done | bytes 131088 | tf_op jit(solution)/shard_map/reduce_scatter | solution.py:282
  980.5 66.3 %reduce-scatter.28.cloned.1.call-done = f32[128,256]{1,0:T(8,128)} async-done(((f32[1024,256]{1,0:T(8,128)}), f32[128,256]{1,0:T(8,128)}) %reduce-scatter.28.cloned.1.call-update) | async-done | bytes 131088 | tf_op jit(solution)/shard_map/reduce_scatter | solution.py:281
  1046.8 66.7 %reduce-scatter.26.cloned.1.call-done = f32[128,256]{1,0:T(8,128)} async-done(((f32[1024,256]{1,0:T(8,128)}), f32[128,256]{1,0:T(8,128)}) %reduce-scatter.26.cloned.1.call-update) | async-done | bytes 131088 | tf_op jit(solution)/shard_map/reduce_scatter | solution.py:280
  (319 shorter events, 304.9 us)
Async XLA Ops:
  21.3 13.7 %all-to-all-start.1 = ((s32[8,128,1]{1,2,0:T(1,128)}), s32[8,128,1]{1,2,0:T(1,128)S(1)}, u32[]{:S(2)}, u32[]{:S(2)}) async-start(s32[8,128,1]{1,2,0:T(1,128)} %bitcast.9), calls=%async_computation.1 | async-start | bytes 8192 | tf_op jit(solution)/shard_map/all_to_all | solution.py:206
  34.9 18.6 %all-to-all-start = ((bf16[8,128,256]{2,1,0:T(8,128)(2,1)}), bf16[8,128,256]{2,1,0:T(8,128)(2,1)S(1)}, u32[]{:S(2)}, u32[]{:S(2)}) async-start(bf16[8,128,256]{2,1,0:T(8,128)(2,1)} %bitcast.6), calls=%async_computation | async-start | bytes 1048576 | tf_op jit(solution)/shard_map/all_to_all | solution.py:203
  39.5 53.7 %all-gather.3.cloned.1.call-start = ((), (), s32[]{:S(2)}) async-start(), calls=%async_computation.20 | async-start | bytes 2621440 | tf_op jit(solution)/shard_map/all_gather | solution.py:68
  70.0 18.3 %all-to-all-start.2 = ((bf16[8,128,256]{2,1,0:T(8,128)(2,1)}), bf16[8,128,256]{2,1,0:T(8,128)(2,1)S(1)}, u32[]{:S(2)}, u32[]{:S(2)}) async-start(bf16[8,128,256]{2,1,0:T(8,128)(2,1)} %bitcast.16), calls=%async_computation.2 | async-start | bytes 1048576 | tf_op jit(solution)/shard_map/all_to_all | solution.py:204
  74.3 96.6 %reduce-scatter.18.cloned.1.call-start = ((), (), s32[]{:S(2)}) async-start(), calls=%async_computation.21 | async-start | bytes 5242880 | tf_op jit(solution)/shard_map/reduce_scatter | solution.py:72
  127.2 111.0 %all-gather.5.cloned.1.call-start = ((), (), s32[]{:S(2)}) async-start(), calls=%async_computation.22 | async-start | bytes 2621440 | tf_op jit(solution)/shard_map/all_gather | solution.py:68
  181.8 115.0 %reduce-scatter.22.cloned.1.call-start = ((), (), s32[]{:S(2)}) async-start(), calls=%async_computation.24 | async-start | bytes 5242880 | tf_op jit(solution)/shard_map/reduce_scatter | solution.py:80
  211.3 13.6 %collective-permute-start.2 = (bf16[1024,256]{1,0:T(8,128)(2,1)S(1)}, bf16[1024,256]{1,0:T(8,128)(2,1)}, u32[]{:S(2)}, u32[]{:S(2)}) collective-permute-start(bf16[1024,256]{1,0:T(8,128)(2,1)S(1)} %gather_fusion.8), channel_id=1, source_target_pairs={{0,3},{1,0},{2,1},{3,2},{4,7},{5,4},{6,5},{7,6},{8,11},{9,8},{10,9... | collective-permute-start | bytes 1572872 | tf_op jit(solution)/shard_map/ppermute | solution.py:20
  254.0 89.7 %reduce-scatter.20.cloned.1.call-start = ((), (), s32[]{:S(2)}) async-start(), calls=%async_computation.23 | async-start | bytes 5242880 | tf_op jit(solution)/shard_map/reduce_scatter | solution.py:72
  259.4 230.9 %reduce-scatter.24.cloned.1.call-start = ((), (), s32[]{:S(2)}) async-start(), calls=%async_computation.25 | async-start | bytes 5242880 | tf_op jit(solution)/shard_map/reduce_scatter | solution.py:80
  346.8 13.8 %collective-permute-start.3 = (bf16[1024,256]{1,0:T(8,128)(2,1)S(1)}, bf16[1024,256]{1,0:T(8,128)(2,1)}, u32[]{:S(2)}, u32[]{:S(2)}) collective-permute-start(bf16[1024,256]{1,0:T(8,128)(2,1)S(1)} %get-tuple-element.275), channel_id=1, source_target_pairs={{0,1},{1,2},{2,3},{3,0},{4,5},{5,6},{6,7},{7,4},{8,9},{9,10},{10,1... | collective-permute-start | bytes 1572872 | tf_op jit(solution)/shard_map/ppermute | solution.py:18
  346.8 14.2 %collective-permute-start.5 = (bf16[1024,256]{1,0:T(8,128)(2,1)S(1)}, bf16[1024,256]{1,0:T(8,128)(2,1)}, u32[]{:S(2)}, u32[]{:S(2)}) collective-permute-start(bf16[1024,256]{1,0:T(8,128)(2,1)S(1)} %get-tuple-element.275), channel_id=1, source_target_pairs={{0,3},{1,0},{2,1},{3,2},{4,7},{5,4},{6,5},{7,6},{8,11},{9,8},{10,9... | collective-permute-start | bytes 1572872 | tf_op jit(solution)/shard_map/ppermute | solution.py:20
  445.9 123.5 %reduce-scatter.42.cloned.1.call-start = ((), (), s32[]{:S(2)}) async-start(), calls=%async_computation.34 | async-start | bytes 147456
  446.7 173.8 %reduce-scatter.40.cloned.1.call-start = ((), (), s32[]{:S(2)}) async-start(), calls=%async_computation.33 | async-start | bytes 147456
  492.9 203.1 %reduce-scatter.38.cloned.1.call-start = ((), (), s32[]{:S(2)}) async-start(), calls=%async_computation.32 | async-start | bytes 3244032 | tf_op jit(solution)/shard_map/reduce_scatter | solution.py:286
  497.5 273.8 %reduce-scatter.36.cloned.1.call-start = ((), (), s32[]{:S(2)}) async-start(), calls=%async_computation.31 | async-start | bytes 3244032 | tf_op jit(solution)/shard_map/reduce_scatter | solution.py:285
  503.7 343.0 %reduce-scatter.34.cloned.1.call-start = ((), (), s32[]{:S(2)}) async-start(), calls=%async_computation.30 | async-start | bytes 3244032 | tf_op jit(solution)/shard_map/reduce_scatter | solution.py:284
  508.5 405.2 %reduce-scatter.32.cloned.1.call-start = ((), (), s32[]{:S(2)}) async-start(), calls=%async_computation.29 | async-start | bytes 1179648 | tf_op jit(solution)/shard_map/reduce_scatter | solution.py:283
  512.8 467.7 %reduce-scatter.30.cloned.1.call-start = ((), (), s32[]{:S(2)}) async-start(), calls=%async_computation.28 | async-start | bytes 1179648 | tf_op jit(solution)/shard_map/reduce_scatter | solution.py:282
  514.7 532.2 %reduce-scatter.28.cloned.1.call-start = ((), (), s32[]{:S(2)}) async-start(), calls=%async_computation.27 | async-start | bytes 1179648 | tf_op jit(solution)/shard_map/reduce_scatter | solution.py:281
  522.6 20.0 %all-to-all-start.3 = ((bf16[8,128,256]{2,1,0:T(8,128)(2,1)}), bf16[8,128,256]{2,1,0:T(8,128)(2,1)S(1)}, u32[]{:S(2)}, u32[]{:S(2)}) async-start(bf16[8,128,256]{2,1,0:T(8,128)(2,1)} %bitcast.209), calls=%async_computation.5 | async-start | bytes 1048576 | tf_op jit(solution)/shard_map/all_to_all | solution.py:291
  528.2 585.3 %reduce-scatter.26.cloned.1.call-start = ((), (), s32[]{:S(2)}) async-start(), calls=%async_computation.26 | async-start | bytes 1179648 | tf_op jit(solution)/shard_map/reduce_scatter | solution.py:280
  542.6 18.6 %all-to-all-start.6 = ((bf16[8,128,256]{2,1,0:T(8,128)(2,1)}), bf16[8,128,256]{2,1,0:T(8,128)(2,1)S(1)}, u32[]{:S(2)}, u32[]{:S(2)}) async-start(bf16[8,128,256]{2,1,0:T(8,128)(2,1)} %bitcast.31), calls=%async_computation.10 | async-start | bytes 1048576 | tf_op jit(solution)/shard_map/all_to_all | solution.py:293
  561.2 60.6 %all-to-all-start.5 = ((bf16[8,128,256]{2,1,0:T(8,128)(2,1)}), bf16[8,128,256]{2,1,0:T(8,128)(2,1)S(1)}, u32[]{:S(2)}, u32[]{:S(2)}) async-start(bf16[8,128,256]{2,1,0:T(8,128)(2,1)} %bitcast.29), calls=%async_computation.9 | async-start | bytes 1048576 | tf_op jit(solution)/shard_map/all_to_all | solution.py:292
  (68 other events, 1684.7 us)
Sparse Core Ops, SparseCore 0:
  65.1 22.1 all-gather.2
  127.3 43.4 reduce-scatter.17
  181.9 23.9 all-gather.4
  254.2 42.6 reduce-scatter.21
  299.2 44.4 reduce-scatter.19
  446.0 44.2 reduce-scatter.23
  493.6 62.5 reduce-scatter.41
  559.5 60.9 reduce-scatter.39
  624.6 71.2 reduce-scatter.37
  699.9 71.3 reduce-scatter.35
  775.4 71.2 reduce-scatter.33
  850.6 63.0 reduce-scatter.31
  918.0 62.4 reduce-scatter.29
  984.4 62.4 reduce-scatter.27
  1051.0 62.4 reduce-scatter.25
